TPU v7x, 512 devices: a whole 4x8x8 slice. The times are simulated.
512 devices in a mesh: gs: 128 (over y, z, core), view: 4 (over x).
Axes of the slice: x: 4, y: 8, z: 8, core: 2. Of those that a mesh axis runs over, the one named last changes fastest.
Arguments:
- features: bfloat16 [131072, 128], P('gs'), may hold values from -6 to 6
- geometry: float32 [4, 9, 131072], P('view', None, 'gs'), as said below
- decoder: bfloat16 [128, 512], replicated, may hold values from -0.5 to 0.5
- teacher: bfloat16 [4, 131072, 512], P('view', 'gs'), may hold values from -3 to 3
- images: float32 [4, 3, 131072], P('view', None, 'gs'), may hold values from 0 to 1
- send_index: int32 [4, 128, 1024], P('view', 'gs'), may hold values from 0 to 1023, as said below
- tile_lists: int32 [4, 512, 8], P('view', 'gs'), may hold values from 0 to 7, as said below
- tile_lengths: int32 [4, 512], P('view', 'gs'), may hold values from 2 to 8
Outputs:
- feature_grad: float32 [131072, 128], P(('gs', 'view'))
- geometry_grad: float32 [4, 9, 131072], P('view', None, 'gs')
- decoder_grad: float32 [128, 512], replicated
Inputs may be any that keep to these rules, and one draw needn't show every extreme that they name: `send_index`: each row (one view, one source device) is a permutation of 0 .. 1023; positions k * 8 to (k + 1) * 8 - 1 hold the Gaussians sent to the device of gs index k. `tile_lists`: the 8 entries of a row are distinct. `geometry`: opacity logits lie in -7.5 .. -4, log conics between -2 log 16 and -2 log 16 + 2 log 4, shears in -2 .. 2, colors in 0 .. 1.
All inputs are finite; a program needn't handle non-finite values.
Results may differ from a plain program's by a relative error of at most 0.0017.
Values may be sent and summed in bfloat16 or wider, within the bound.
A program may use at most 64 MiB of HBM per device.

v0:
```python
import math
import jax
import jax.numpy as jnp
from jax import lax
from jax.sharding import PartitionSpec as P

FEAT = 128
CT = 512
TS = 16
BLK = 128
LIST = 8


def composite(tile_geo, alive_mask, pixel_x, pixel_y):
    delta_x = pixel_x[:, None] - tile_geo[0][None, :]
    delta_y = pixel_y[:, None] - tile_geo[1][None, :]
    conic_a = jnp.exp(tile_geo[2])
    conic_c = jnp.exp(tile_geo[3])
    conic_b = 0.8 * jnp.tanh(tile_geo[4]) * jnp.exp(0.5 * (tile_geo[2] + tile_geo[3]))
    exponent = -0.5 * (
        conic_a * delta_x * delta_x
        + 2.0 * conic_b * delta_x * delta_y
        + conic_c * delta_y * delta_y
    )
    opacity = alive_mask * jax.nn.sigmoid(tile_geo[5])
    alpha_val = opacity[None, :] * jnp.exp(exponent)
    log_keep = jnp.log1p(-alpha_val)
    pixel_count = pixel_x.shape[0]
    blocked = log_keep.reshape(pixel_count, LIST, BLK)
    inner = jnp.cumsum(blocked, axis=2) - blocked
    block_sums = jnp.sum(blocked, axis=2)
    outer = jnp.cumsum(block_sums, axis=1) - block_sums
    before = (inner + outer[:, :, None]).reshape(pixel_count, LIST * BLK)
    weights = alpha_val * jnp.exp(before)
    pixel_color = jnp.einsum("pi,ci->cp", weights, tile_geo[6:9], precision=lax.Precision.HIGHEST)
    return (weights, pixel_color)


def device_terms(
    recv_geo, recv_feat, decoder, teacher_dev, images_dev, lists, lengths, shard_index
):
    nblocks = recv_feat.shape[0] // BLK
    tile_pixels = TS * TS
    geo_blocks = recv_geo.reshape(9, nblocks, BLK)
    feat_blocks = recv_feat.reshape(nblocks, BLK, FEAT)
    within = jnp.arange(tile_pixels, dtype=jnp.int32)
    block_range = jnp.arange(nblocks, dtype=jnp.int32)
    slot_range = jnp.arange(LIST, dtype=jnp.int32)

    def tile_step(totals, tile_index):
        decoder_sum, geo_acc, feat_acc = totals
        block_ids = lists[tile_index]
        count = lengths[tile_index]
        alive_mask = jnp.broadcast_to(
            (slot_range < count).astype(jnp.float32)[:, None], (LIST, BLK)
        ).reshape(LIST * BLK)
        tile_geo = jnp.take(geo_blocks, block_ids, axis=1).reshape(9, LIST * BLK)
        feat_tile = jnp.take(feat_blocks, block_ids, axis=0).reshape(LIST * BLK, FEAT)
        column = 2 * TS * (shard_index % 30) + TS * (tile_index % 2) + within % TS
        row_index = 2 * TS * (shard_index // 30) + TS * (tile_index // 2) + within // TS
        pixel_x = column.astype(jnp.float32) + 0.5
        pixel_y = row_index.astype(jnp.float32) + 0.5
        (weights, pixel_color), pullback = jax.vjp(
            lambda geo_part: composite(geo_part, alive_mask, pixel_x, pixel_y), tile_geo
        )
        weight_b = weights.astype(jnp.bfloat16)
        rendered = jnp.dot(weight_b, feat_tile, preferred_element_type=jnp.float32).astype(
            jnp.bfloat16
        )
        pred = jnp.dot(rendered, decoder, preferred_element_type=jnp.float32)
        teacher_rows = lax.dynamic_slice_in_dim(
            teacher_dev, tile_index * tile_pixels, tile_pixels, 0
        )
        error_feat = pred - teacher_rows.astype(jnp.float32)
        gpred = (error_feat / jnp.sqrt(error_feat * error_feat + 0.04)).astype(jnp.bfloat16)
        grender = lax.dot_general(
            gpred, decoder, (((1,), (1,)), ((), ())), preferred_element_type=jnp.float32
        ).astype(jnp.bfloat16)
        decoder_sum = decoder_sum + lax.dot_general(
            rendered, gpred, (((0,), (0,)), ((), ())), preferred_element_type=jnp.float32
        )
        image_cols = lax.dynamic_slice_in_dim(images_dev, tile_index * tile_pixels, tile_pixels, 1)
        error_color = pixel_color - image_cols
        gcolor = error_color / jnp.sqrt(error_color * error_color + 0.04)
        gweight = lax.dot_general(
            grender, feat_tile, (((1,), (1,)), ((), ())), preferred_element_type=jnp.float32
        )
        gfeat_tile = lax.dot_general(
            weight_b, grender, (((0,), (0,)), ((), ())), preferred_element_type=jnp.float32
        )
        (ggeo_tile,) = pullback((gweight, gcolor))
        hits = (block_ids[:, None] == block_range[None, :]).astype(jnp.float32)
        geo_acc = geo_acc + jnp.einsum(
            "clb,ln->cnb", ggeo_tile.reshape(9, LIST, BLK), hits, precision=lax.Precision.HIGHEST
        )
        feat_acc = feat_acc + jnp.einsum(
            "ln,lbf->nbf",
            hits,
            gfeat_tile.reshape(LIST, BLK, FEAT),
            precision=lax.Precision.HIGHEST,
        )
        return ((decoder_sum, geo_acc, feat_acc), None)

    start_totals = (
        jnp.zeros((FEAT, CT), jnp.float32),
        jnp.zeros((9, nblocks, BLK), jnp.float32),
        jnp.zeros((nblocks, BLK, FEAT), jnp.float32),
    )
    tile_range = jnp.arange(lists.shape[0], dtype=jnp.int32)
    (decoder_sum, geo_acc, feat_acc), _ = lax.scan(tile_step, start_totals, tile_range)
    return (decoder_sum, geo_acc.reshape(9, nblocks * BLK), feat_acc.reshape(nblocks * BLK, FEAT))


def on_device(features, geometry, decoder, teacher, images, send_index, tile_lists, tile_lengths):
    send_order = send_index[0, 0]
    shard_index = lax.axis_index("gs")
    geo_send = jnp.take(geometry[0], send_order, axis=1)
    recv_geo = lax.all_to_all(geo_send, "gs", split_axis=1, concat_axis=1, tiled=True)
    feat_send = jnp.take(features, send_order, axis=0)
    recv_feat = lax.all_to_all(feat_send, "gs", split_axis=0, concat_axis=0, tiled=True)
    decoder_sum, geo_acc, feat_acc = device_terms(
        recv_geo,
        recv_feat,
        decoder,
        teacher[0],
        images[0],
        tile_lists[0],
        tile_lengths[0],
        shard_index,
    )
    returned_geo = lax.all_to_all(geo_acc, "gs", split_axis=1, concat_axis=1, tiled=True)
    returned_feat = lax.all_to_all(feat_acc, "gs", split_axis=0, concat_axis=0, tiled=True)
    geo_own = jnp.zeros_like(returned_geo).at[:, send_order].set(returned_geo)
    feat_own = jnp.zeros_like(returned_feat).at[send_order].set(returned_feat)
    quarter = feat_own.shape[0] // lax.axis_size("view")
    summed = lax.psum(feat_own, "view")
    feature_grad = lax.dynamic_slice_in_dim(summed, lax.axis_index("view") * quarter, quarter, 0)
    pixel_total = lax.axis_size("gs") * lax.axis_size("view") * tile_lists.shape[1] * TS * TS
    decoder_grad = lax.psum(decoder_sum, ("gs", "view")) * (1.0 / math.sqrt(pixel_total))
    return (feature_grad, geo_own[None], decoder_grad)


def solution(mesh):
    placed = (
        P("gs", None),
        P("view", None, "gs"),
        P(),
        P("view", "gs", None),
        P("view", None, "gs"),
        P("view", "gs", None),
        P("view", "gs", None),
        P("view", "gs"),
    )
    return jax.shard_map(
        on_device,
        mesh=mesh,
        in_specs=placed,
        out_specs=(P(("gs", "view"), None), P("view", None, "gs"), P()),
        check_vma=False,
    )
```

profile of v0, /device:TPU:8, one launch (start us, length us, event | category | flops | bytes accessed | tf_op | source)
XLA Modules:
  0.0 610.4 jit_solution(10011325874883574381)
XLA Ops:
  10.2 2.8 gather_fusion.2
  14.1 17.4 %all-to-all-start = ((f32[9,128,8]{0,2,1:T(8,128)}), f32[9,128,8]{0,2,1:T(8,128)S(1)}, u32[]{:S(2)}, u32[]{:S(2)}) async-start(f32[9,128,8]{0,2,1:T(8,128)} %bitcast_select_fusion.1), calls=%async_computation | async-start | bytes 1048576 | tf_op jit(solution)/shard_map/all_to_all | solution.py:118
  31.5 3.2 gather_fusion.3
  35.6 16.2 %all-to-all-done = f32[9,128,8]{0,2,1:T(8,128)S(1)} async-done(((f32[9,128,8]{0,2,1:T(8,128)}), f32[9,128,8]{0,2,1:T(8,128)S(1)}, u32[]{:S(2)}, u32[]{:S(2)}) %all-to-all-start) | async-done | bytes 36896 | tf_op jit(solution)/shard_map/all_to_all | solution.py:118
  51.8 6.5 %all-to-all-start.1 = ((bf16[128,8,128]{2,1,0:T(8,128)(2,1)}), bf16[128,8,128]{2,1,0:T(8,128)(2,1)S(1)}, u32[]{:S(2)}, u32[]{:S(2)}) async-start(bf16[128,8,128]{2,1,0:T(8,128)(2,1)} %bitcast_select_fusion.2), calls=%async_computation.1 | async-start | bytes 524288 | tf_op jit(solution)/shard_map/all_to_all | solution.py:120
  60.4 12.6 %all-to-all-done.1 = bf16[128,8,128]{2,1,0:T(8,128)(2,1)S(1)} async-done(((bf16[128,8,128]{2,1,0:T(8,128)(2,1)}), bf16[128,8,128]{2,1,0:T(8,128)(2,1)S(1)}, u32[]{:S(2)}, u32[]{:S(2)}) %all-to-all-start.1) | async-done | bytes 262176 | tf_op jit(solution)/shard_map/all_to_all | solution.py:120
  73.7 187.1 %while.21 = (s32[]{:T(128)}, f32[128,512]{1,0:T(8,128)}, f32[9,8,128]{2,1,0:T(8,128)}, f32[8,128,128]{2,0,1:T(8,128)}, s32[4]{0:T(128)S(1)}, /*index=5*/s32[4]{0...) while((s32[]{:T(128)}, f32[128,512]{1,0:T(8,128)}, ...), condition=%wide.region_13.14_spmd.clone.clone, body=%wide.region_0.13_spmd.clone.clone.sunk | while | flops 448201472 | bytes 62394652 | solution.py:110
  82.8 1.4 gather_fusion
  89.3 2.2 exponential_multiply_fusion.2
  91.6 1.1 fusion.164
  93.2 1.2 convert_bitcast_fusion.2
  95.6 1.4 rsqrt_multiply_fusion.2
  97.1 1.8 fusion.171
  98.9 1.2 multiply_convert_fusion.2
  101.7 1.2 convolution_add_fusion.8
  105.5 1.5 copy.140
  107.0 3.4 fusion.167
  110.4 1.5 copy.141
  114.7 2.3 fusion.168
  128.7 1.4 gather_fusion
  135.2 2.2 exponential_multiply_fusion.2
  137.5 1.1 fusion.164
  139.1 1.2 convert_bitcast_fusion.2
  141.6 1.4 rsqrt_multiply_fusion.2
  143.1 1.8 fusion.171
  144.9 1.2 multiply_convert_fusion.2
  147.6 2.3 convolution_add_fusion.8
  152.6 1.5 copy.140
  154.0 3.4 fusion.167
  157.4 1.5 copy.141
  161.7 2.3 fusion.168
  175.7 1.4 gather_fusion
  182.3 2.2 exponential_multiply_fusion.2
  186.2 1.2 convert_bitcast_fusion.2
  188.6 1.5 rsqrt_multiply_fusion.2
  190.1 1.8 fusion.171
  191.9 1.2 multiply_convert_fusion.2
  194.7 2.3 convolution_add_fusion.8
  199.6 1.5 copy.140
  201.1 3.4 fusion.167
  204.4 1.5 copy.141
  208.8 2.3 fusion.168
  222.8 1.4 gather_fusion
  229.3 2.2 exponential_multiply_fusion.2
  233.2 1.2 convert_bitcast_fusion.2
  235.6 1.5 rsqrt_multiply_fusion.2
  237.1 1.8 fusion.171
  239.0 1.2 multiply_convert_fusion.2
  241.7 2.3 convolution_add_fusion.8
  246.6 1.5 copy.140
  248.1 3.4 fusion.167
  251.5 1.5 copy.141
  255.8 2.3 fusion.168
  260.8 1.9 copy.80
  262.7 6.5 %all-to-all-start.2 = ((f32[128,8,128]{2,1,0:T(8,128)}), f32[128,8,128]{2,1,0:T(8,128)S(1)}, u32[]{:S(2)}, u32[]{:S(2)}) async-start(f32[128,8,128]{2,1,0:T(8,128)} %bitcast.11), calls=%async_computation.2 | async-start | bytes 1048576 | tf_op jit(solution)/shard_map/all_to_all | solution.py:132
  270.0 19.5 %all-to-all-done.2 = f32[128,8,128]{2,1,0:T(8,128)S(1)} async-done(((f32[128,8,128]{2,1,0:T(8,128)}), f32[128,8,128]{2,1,0:T(8,128)S(1)}, u32[]{:S(2)}, u32[]{:S(2)}) %all-to-all-start.2) | async-done | bytes 524320 | tf_op jit(solution)/shard_map/all_to_all | solution.py:132
  289.5 4.0 scatter_custom_fusion
  295.4 6.4 %all-to-all-start.3 = ((f32[9,128,8]{0,2,1:T(8,128)}), f32[9,128,8]{0,2,1:T(8,128)S(1)}, u32[]{:S(2)}, u32[]{:S(2)}) async-start(f32[9,128,8]{0,2,1:T(8,128)} %bitcast.13), calls=%async_computation.3 | async-start | bytes 1048576 | tf_op jit(solution)/shard_map/all_to_all | solution.py:131
  301.7 20.4 %all-to-all-done.3 = f32[9,128,8]{0,2,1:T(8,128)S(1)} async-done(((f32[9,128,8]{0,2,1:T(8,128)}), f32[9,128,8]{0,2,1:T(8,128)S(1)}, u32[]{:S(2)}, u32[]{:S(2)}) %all-to-all-start.3) | async-done | bytes 36896 | tf_op jit(solution)/shard_map/all_to_all | solution.py:131
  322.2 3.4 scatter_custom_fusion.1
  326.4 222.5 %all-reduce.14.cloned.1.call-done = f32[128,512]{1,0:T(8,128)} async-done(((f32[128,512]{1,0:T(8,128)}), f32[128,512]{1,0:T(8,128)}) %all-reduce.14.cloned.1.call-update) | async-done | bytes 262160 | tf_op jit(solution)/shard_map/psum | solution.py:139
  548.8 1.7 broadcast_multiply_fusion.2
  550.5 51.4 %all-reduce.12.cloned.1.call-done = f32[1024,128]{1,0:T(8,128)} async-done(((f32[1024,128]{1,0:T(8,128)}), f32[1024,128]{1,0:T(8,128)}) %all-reduce.12.cloned.1.call-update) | async-done | bytes 524304 | tf_op jit(solution)/shard_map/psum | solution.py:136
  602.0 1.6 constant_dynamic-slice_fusion.1
  (485 shorter events, 96.0 us)
Async XLA Ops:
  7.2 24.3 %copy-start = (bf16[1024,128]{1,0:T(8,128)(2,1)S(1)}, bf16[1024,128]{1,0:T(8,128)(2,1)}, u32[]{:S(2)}) copy-start(bf16[1024,128]{1,0:T(8,128)(2,1)} %param.10) | copy-start | bytes 786436
  14.1 37.7 %all-to-all-start = ((f32[9,128,8]{0,2,1:T(8,128)}), f32[9,128,8]{0,2,1:T(8,128)S(1)}, u32[]{:S(2)}, u32[]{:S(2)}) async-start(f32[9,128,8]{0,2,1:T(8,128)} %bitcast_select_fusion.1), calls=%async_computation | async-start | bytes 1048576 | tf_op jit(solution)/shard_map/all_to_all | solution.py:118
  51.8 21.3 %all-to-all-start.1 = ((bf16[128,8,128]{2,1,0:T(8,128)(2,1)}), bf16[128,8,128]{2,1,0:T(8,128)(2,1)S(1)}, u32[]{:S(2)}, u32[]{:S(2)}) async-start(bf16[128,8,128]{2,1,0:T(8,128)(2,1)} %bitcast_select_fusion.2), calls=%async_computation.1 | async-start | bytes 524288 | tf_op jit(solution)/shard_map/all_to_all | solution.py:120
  73.7 13.7 %copy-start.8 = (bf16[8,128,128]{2,1,0:T(8,128)(2,1)}, bf16[8,128,128]{2,1,0:T(8,128)(2,1)S(1)}, u32[]{:S(2)}) copy-start(bf16[8,128,128]{2,1,0:T(8,128)(2,1)S(1)} %get-tuple-element.843) | copy-start | bytes 786436 | tf_op jit(solution)/shard_map/while
  81.3 22.9 %copy-start.21 = (f32[256]{0:T(256)}, f32[256]{0:T(256)S(1)}, u32[]{:S(2)}) copy-start(f32[256]{0:T(256)S(1)} %get-tuple-element.768) | copy-start | bytes 3076 | tf_op jit(solution)/shard_map/while
  81.3 22.9 %copy-start.23 = (f32[256]{0:T(256)}, f32[256]{0:T(256)S(1)}, u32[]{:S(2)}) copy-start(f32[256]{0:T(256)S(1)} %get-tuple-element.765) | copy-start | bytes 3076 | tf_op jit(solution)/shard_map/while
  82.0 19.6 %copy-start.28 = (s32[8]{0:T(128)}, s32[8]{0:T(128)S(1)}, u32[]{:S(2)}) copy-start(s32[8]{0:T(128)S(1)} %get-tuple-element.785) | copy-start | bytes 100 | tf_op jit(solution)/shard_map/while
  84.2 18.9 %copy-start.5 = (f32[9,8,128]{2,0,1:T(8,128)}, f32[9,8,128]{2,0,1:T(8,128)S(1)}, u32[]{:S(2)}) copy-start(f32[9,8,128]{2,0,1:T(8,128)S(1)} %select_bitcast_fusion.2) | copy-start | bytes 110596 | tf_op jit(solution)/shard_map/while
  84.9 19.4 %copy-start.11 = (f32[1,8,128]{2,0,1:T(1,128)}, f32[1,8,128]{2,0,1:T(1,128)S(1)}, u32[]{:S(2)}) copy-start(f32[1,8,128]{2,0,1:T(1,128)S(1)} %get-tuple-element.769) | copy-start | bytes 12292 | tf_op jit(solution)/shard_map/while
  85.5 18.8 %copy-start.16 = (f32[1024]{0:T(1024)}, f32[1024]{0:T(1024)S(1)}, u32[]{:S(2)}) copy-start(f32[1024]{0:T(1024)S(1)} %bitcast_multiply_fusion.8) | copy-start | bytes 12292 | tf_op jit(solution)/shard_map/while
  111.9 2.1 copy-start.3
  114.7 2.3 copy-start.15
  114.7 2.3 copy-start.26
  114.7 2.4 copy-start.27
  114.7 3.3 copy-start.25
  117.0 2.6 copy-start.9
  119.6 13.7 %copy-start.8 = (bf16[8,128,128]{2,1,0:T(8,128)(2,1)}, bf16[8,128,128]{2,1,0:T(8,128)(2,1)S(1)}, u32[]{:S(2)}) copy-start(bf16[8,128,128]{2,1,0:T(8,128)(2,1)S(1)} %get-tuple-element.843) | copy-start | bytes 786436 | tf_op jit(solution)/shard_map/while
  127.3 24.0 %copy-start.21 = (f32[256]{0:T(256)}, f32[256]{0:T(256)S(1)}, u32[]{:S(2)}) copy-start(f32[256]{0:T(256)S(1)} %get-tuple-element.768) | copy-start | bytes 3076 | tf_op jit(solution)/shard_map/while
  127.3 24.0 %copy-start.23 = (f32[256]{0:T(256)}, f32[256]{0:T(256)S(1)}, u32[]{:S(2)}) copy-start(f32[256]{0:T(256)S(1)} %get-tuple-element.765) | copy-start | bytes 3076 | tf_op jit(solution)/shard_map/while
  128.0 19.6 %copy-start.28 = (s32[8]{0:T(128)}, s32[8]{0:T(128)S(1)}, u32[]{:S(2)}) copy-start(s32[8]{0:T(128)S(1)} %get-tuple-element.785) | copy-start | bytes 100 | tf_op jit(solution)/shard_map/while
  130.2 20.0 %copy-start.5 = (f32[9,8,128]{2,0,1:T(8,128)}, f32[9,8,128]{2,0,1:T(8,128)S(1)}, u32[]{:S(2)}) copy-start(f32[9,8,128]{2,0,1:T(8,128)S(1)} %select_bitcast_fusion.2) | copy-start | bytes 110596 | tf_op jit(solution)/shard_map/while
  130.8 20.5 %copy-start.11 = (f32[1,8,128]{2,0,1:T(1,128)}, f32[1,8,128]{2,0,1:T(1,128)S(1)}, u32[]{:S(2)}) copy-start(f32[1,8,128]{2,0,1:T(1,128)S(1)} %get-tuple-element.769) | copy-start | bytes 12292 | tf_op jit(solution)/shard_map/while
  131.4 19.9 %copy-start.16 = (f32[1024]{0:T(1024)}, f32[1024]{0:T(1024)S(1)}, u32[]{:S(2)}) copy-start(f32[1024]{0:T(1024)S(1)} %bitcast_multiply_fusion.8) | copy-start | bytes 12292 | tf_op jit(solution)/shard_map/while
  147.3 2.6 copy-start.7
  147.6 2.3 copy-start.4
  161.7 2.3 copy-start.15
  161.7 2.3 copy-start.26
  161.7 2.4 copy-start.27
  161.7 3.3 copy-start.25
  164.0 2.6 copy-start.9
  166.6 13.7 %copy-start.8 = (bf16[8,128,128]{2,1,0:T(8,128)(2,1)}, bf16[8,128,128]{2,1,0:T(8,128)(2,1)S(1)}, u32[]{:S(2)}) copy-start(bf16[8,128,128]{2,1,0:T(8,128)(2,1)S(1)} %get-tuple-element.843) | copy-start | bytes 786436 | tf_op jit(solution)/shard_map/while
  174.3 24.0 %copy-start.21 = (f32[256]{0:T(256)}, f32[256]{0:T(256)S(1)}, u32[]{:S(2)}) copy-start(f32[256]{0:T(256)S(1)} %get-tuple-element.768) | copy-start | bytes 3076 | tf_op jit(solution)/shard_map/while
  174.3 24.0 %copy-start.23 = (f32[256]{0:T(256)}, f32[256]{0:T(256)S(1)}, u32[]{:S(2)}) copy-start(f32[256]{0:T(256)S(1)} %get-tuple-element.765) | copy-start | bytes 3076 | tf_op jit(solution)/shard_map/while
  175.0 19.6 %copy-start.28 = (s32[8]{0:T(128)}, s32[8]{0:T(128)S(1)}, u32[]{:S(2)}) copy-start(s32[8]{0:T(128)S(1)} %get-tuple-element.785) | copy-start | bytes 100 | tf_op jit(solution)/shard_map/while
  177.2 20.0 %copy-start.5 = (f32[9,8,128]{2,0,1:T(8,128)}, f32[9,8,128]{2,0,1:T(8,128)S(1)}, u32[]{:S(2)}) copy-start(f32[9,8,128]{2,0,1:T(8,128)S(1)} %select_bitcast_fusion.2) | copy-start | bytes 110596 | tf_op jit(solution)/shard_map/while
  177.8 20.5 %copy-start.11 = (f32[1,8,128]{2,0,1:T(1,128)}, f32[1,8,128]{2,0,1:T(1,128)S(1)}, u32[]{:S(2)}) copy-start(f32[1,8,128]{2,0,1:T(1,128)S(1)} %get-tuple-element.769) | copy-start | bytes 12292 | tf_op jit(solution)/shard_map/while
  178.4 19.9 %copy-start.16 = (f32[1024]{0:T(1024)}, f32[1024]{0:T(1024)S(1)}, u32[]{:S(2)}) copy-start(f32[1024]{0:T(1024)S(1)} %bitcast_multiply_fusion.8) | copy-start | bytes 12292 | tf_op jit(solution)/shard_map/while
  194.3 2.6 copy-start.7
  194.6 2.3 copy-start.4
  205.9 2.1 copy-start.3
  208.7 2.3 copy-start.15
  208.7 2.3 copy-start.26
  208.7 2.4 copy-start.27
  208.7 3.3 copy-start.25
  211.0 2.6 copy-start.9
  213.7 13.7 %copy-start.8 = (bf16[8,128,128]{2,1,0:T(8,128)(2,1)}, bf16[8,128,128]{2,1,0:T(8,128)(2,1)S(1)}, u32[]{:S(2)}) copy-start(bf16[8,128,128]{2,1,0:T(8,128)(2,1)S(1)} %get-tuple-element.843) | copy-start | bytes 786436 | tf_op jit(solution)/shard_map/while
  221.3 24.0 %copy-start.21 = (f32[256]{0:T(256)}, f32[256]{0:T(256)S(1)}, u32[]{:S(2)}) copy-start(f32[256]{0:T(256)S(1)} %get-tuple-element.768) | copy-start | bytes 3076 | tf_op jit(solution)/shard_map/while
  221.3 24.0 %copy-start.23 = (f32[256]{0:T(256)}, f32[256]{0:T(256)S(1)}, u32[]{:S(2)}) copy-start(f32[256]{0:T(256)S(1)} %get-tuple-element.765) | copy-start | bytes 3076 | tf_op jit(solution)/shard_map/while
  222.0 19.6 %copy-start.28 = (s32[8]{0:T(128)}, s32[8]{0:T(128)S(1)}, u32[]{:S(2)}) copy-start(s32[8]{0:T(128)S(1)} %get-tuple-element.785) | copy-start | bytes 100 | tf_op jit(solution)/shard_map/while
  224.2 20.0 %copy-start.5 = (f32[9,8,128]{2,0,1:T(8,128)}, f32[9,8,128]{2,0,1:T(8,128)S(1)}, u32[]{:S(2)}) copy-start(f32[9,8,128]{2,0,1:T(8,128)S(1)} %select_bitcast_fusion.2) | copy-start | bytes 110596 | tf_op jit(solution)/shard_map/while
  224.9 20.5 %copy-start.11 = (f32[1,8,128]{2,0,1:T(1,128)}, f32[1,8,128]{2,0,1:T(1,128)S(1)}, u32[]{:S(2)}) copy-start(f32[1,8,128]{2,0,1:T(1,128)S(1)} %get-tuple-element.769) | copy-start | bytes 12292 | tf_op jit(solution)/shard_map/while
  225.5 19.9 %copy-start.16 = (f32[1024]{0:T(1024)}, f32[1024]{0:T(1024)S(1)}, u32[]{:S(2)}) copy-start(f32[1024]{0:T(1024)S(1)} %bitcast_multiply_fusion.8) | copy-start | bytes 12292 | tf_op jit(solution)/shard_map/while
  241.4 2.6 copy-start.7
  241.7 2.3 copy-start.4
  253.0 2.1 copy-start.3
  255.8 2.3 copy-start.15
  255.8 2.3 copy-start.26
  255.8 2.4 copy-start.27
  255.8 3.3 copy-start.25
  258.1 2.6 copy-start.9
  262.7 26.8 %all-to-all-start.2 = ((f32[128,8,128]{2,1,0:T(8,128)}), f32[128,8,128]{2,1,0:T(8,128)S(1)}, u32[]{:S(2)}, u32[]{:S(2)}) async-start(f32[128,8,128]{2,1,0:T(8,128)} %bitcast.11), calls=%async_computation.2 | async-start | bytes 1048576 | tf_op jit(solution)/shard_map/all_to_all | solution.py:132
  269.2 279.6 %all-reduce.14.cloned.1.call-start = ((), (), s32[]{:S(2)}) async-start(), calls=%async_computation.5 | async-start | bytes 524288 | tf_op jit(solution)/shard_map/psum | solution.py:139
  269.9 332.0 %all-reduce.12.cloned.1.call-start = ((), (), s32[]{:S(2)}) async-start(), calls=%async_computation.4 | async-start | bytes 1048576 | tf_op jit(solution)/shard_map/psum | solution.py:136
  295.4 26.8 %all-to-all-start.3 = ((f32[9,128,8]{0,2,1:T(8,128)}), f32[9,128,8]{0,2,1:T(8,128)S(1)}, u32[]{:S(2)}, u32[]{:S(2)}) async-start(f32[9,128,8]{0,2,1:T(8,128)} %bitcast.13), calls=%async_computation.3 | async-start | bytes 1048576 | tf_op jit(solution)/shard_map/all_to_all | solution.py:131
  (73 other events, 68.1 us)
Sparse Core Ops, SparseCore 0:
  275.6 273.1 all-reduce.13
  551.3 50.6 all-reduce.11
where the time goes:
time: 613 us; the launch traced here: 610 us
  waiting for transfers between devices  343 us (56%)
  local copies, waits for them, and re-layouts  79.9 us (13%)
  other arithmetic  76.6 us (12%)
  matrix products  39.1 us (6%)
  starting transfers between devices  36.8 us (6%)
  loops' own time  20.3 us (3%)
  between operations  14.3 us (2%)
    psum x1, waiting for transfers between devices, on_device(): lax.psum(decoder_sum, ('gs', 'view')) * (1.0 / math.sqrt(pixel_total))  222 us
    psum x1, waiting for transfers between devices, on_device(): summed = lax.psum(feat_own, 'view')  51.4 us
    another operation x8, other arithmetic, composite(): inner = jnp.cumsum(blocked, axis=2) - blocked  22.4 us
    all_to_all x1, waiting for transfers between devices, on_device(): lax.all_to_all(geo_acc, 'gs', split_axis=1, concat_axis=1, tiled=True)  20.4 us
    another operation x1, loops' own time, device_terms(): lax.scan(tile_step, start_totals, tile_range)  20.3 us
    all_to_all x1, waiting for transfers between devices, on_device(): lax.all_to_all(feat_acc, 'gs', split_axis=0, concat_axis=0, tiled=True)  19.5 us
    while x264, local copies, waits for them, and re-layouts  19.3 us
    all_to_all x1, starting transfers between devices, on_device(): lax.all_to_all(geo_send, 'gs', split_axis=1, concat_axis=1, tiled=True)  17.4 us
  transfers between devices with their start and end apart: 6, of which 6 were waited for; matrix products, arithmetic and copies ran while one was open for 3% of the time, Pallas kernels for 0%

commit v1 on v0

--- a/solution.py
+++ b/solution.py
@@ -133,7 +133,9 @@
     geo_own = jnp.zeros_like(returned_geo).at[:, send_order].set(returned_geo)
     feat_own = jnp.zeros_like(returned_feat).at[send_order].set(returned_feat)
     quarter = feat_own.shape[0] // lax.axis_size("view")
-    summed = lax.psum(feat_own, "view")
+    summed = feat_own
+    for hop in (1, 2):
+        summed = summed + lax.ppermute(summed, "view", [(dev, dev ^ hop) for dev in range(4)])
     feature_grad = lax.dynamic_slice_in_dim(summed, lax.axis_index("view") * quarter, quarter, 0)
     pixel_total = lax.axis_size("gs") * lax.axis_size("view") * tile_lists.shape[1] * TS * TS
     decoder_grad = lax.psum(decoder_sum, ("gs", "view")) * (1.0 / math.sqrt(pixel_total))

time: 613 us -> 586 us (0.956)
  the two profiles are of different devices: /device:TPU:8 before, /device:TPU:23 now
where the time goes in v1:
time: 586 us; the launch traced here: 583 us
  waiting for transfers between devices  292 us (50%)
  other arithmetic  77.3 us (13%)
  local copies, waits for them, and re-layouts  73 us (12%)
  starting transfers between devices  41.9 us (7%)
  matrix products  39.3 us (7%)
  blocking collectives  25.3 us (4%)
  loops' own time  20.6 us (4%)
  between operations  14.3 us (2%)
    psum x1, waiting for transfers between devices, on_device(): lax.psum(decoder_sum, ('gs', 'view')) * (1.0 / math.sqrt(pixel_total))  237 us
    all_to_all x1, blocking collectives, on_device(): lax.all_to_all(feat_acc, 'gs', split_axis=0, concat_axis=0, tiled=True)  25.3 us
    another operation x8, other arithmetic, composite(): inner = jnp.cumsum(blocked, axis=2) - blocked  22.4 us
    another operation x1, loops' own time, device_terms(): lax.scan(tile_step, start_totals, tile_range)  20.6 us
    while x280, local copies, waits for them, and re-layouts  19.2 us
    all_to_all x1, waiting for transfers between devices, on_device(): lax.all_to_all(geo_acc, 'gs', split_axis=1, concat_axis=1, tiled=True)  18 us
    all_to_all x1, starting transfers between devices, on_device(): lax.all_to_all(geo_send, 'gs', split_axis=1, concat_axis=1, tiled=True)  17.7 us
    dot_general x12, matrix products, composite(): jnp.einsum('pi,ci->cp', weights, tile_geo[6:9], precision=lax.Precision.H...  17.3 us
  transfers between devices with their start and end apart: 6, of which 5 were waited for; matrix products, arithmetic and copies ran while one was open for 2% of the time, Pallas kernels for 0%

profile of v1, /device:TPU:23, one launch (start us, length us, event | category | flops | bytes accessed | tf_op | source)
XLA Modules:
  0.0 583.4 jit_solution(10601757120363102289)
XLA Ops:
  10.2 2.8 gather_fusion.2
  14.1 17.7 %all-to-all-start = ((f32[9,128,8]{0,2,1:T(8,128)}), f32[9,128,8]{0,2,1:T(8,128)S(1)}, u32[]{:S(2)}, u32[]{:S(2)}) async-start(f32[9,128,8]{0,2,1:T(8,128)} %bitcast_select_fusion.1), calls=%async_computation | async-start | bytes 1048576 | tf_op jit(solution)/shard_map/all_to_all | solution.py:118
  31.7 3.2 gather_fusion.3
  35.9 13.8 %all-to-all-done = f32[9,128,8]{0,2,1:T(8,128)S(1)} async-done(((f32[9,128,8]{0,2,1:T(8,128)}), f32[9,128,8]{0,2,1:T(8,128)S(1)}, u32[]{:S(2)}, u32[]{:S(2)}) %all-to-all-start) | async-done | bytes 36896 | tf_op jit(solution)/shard_map/all_to_all | solution.py:118
  49.6 8.9 %all-to-all-start.1 = ((bf16[128,8,128]{2,1,0:T(8,128)(2,1)}), bf16[128,8,128]{2,1,0:T(8,128)(2,1)S(1)}, u32[]{:S(2)}, u32[]{:S(2)}) async-start(bf16[128,8,128]{2,1,0:T(8,128)(2,1)} %bitcast_select_fusion.2), calls=%async_computation.1 | async-start | bytes 524288 | tf_op jit(solution)/shard_map/all_to_all | solution.py:120
  60.1 11.6 %all-to-all-done.1 = bf16[128,8,128]{2,1,0:T(8,128)(2,1)S(1)} async-done(((bf16[128,8,128]{2,1,0:T(8,128)(2,1)}), bf16[128,8,128]{2,1,0:T(8,128)(2,1)S(1)}, u32[]{:S(2)}, u32[]{:S(2)}) %all-to-all-start.1) | async-done | bytes 262176 | tf_op jit(solution)/shard_map/all_to_all | solution.py:120
  72.3 184.3 %while.21 = (s32[]{:T(128)}, f32[128,512]{1,0:T(8,128)}, f32[9,8,128]{2,1,0:T(8,128)}, f32[8,128,128]{2,0,1:T(8,128)}, s32[4]{0:T(128)S(1)}, /*index=5*/s32[4]{0...) while((s32[]{:T(128)}, f32[128,512]{1,0:T(8,128)}, ...), condition=%wide.region_13.14_spmd.clone.clone, body=%wide.region_0.13_spmd.clone.clone.sunk | while | flops 448201472 | bytes 62689620 | solution.py:110
  87.2 2.2 exponential_multiply_fusion.2
  89.5 1.1 fusion.164
  91.1 1.2 convert_bitcast_fusion.2
  93.6 1.4 rsqrt_multiply_fusion.2
  95.0 1.8 fusion.171
  96.9 1.2 multiply_convert_fusion.2
  99.6 1.2 convolution_add_fusion.8
  101.1 1.1 convolution_add_fusion.7
  103.5 1.5 copy.140
  105.0 3.4 fusion.167
  108.4 1.5 copy.141
  112.6 2.3 fusion.168
  132.4 2.2 exponential_multiply_fusion.2
  134.7 1.1 fusion.164
  136.3 1.2 convert_bitcast_fusion.2
  138.8 1.4 rsqrt_multiply_fusion.2
  140.2 1.8 fusion.171
  142.1 1.2 multiply_convert_fusion.2
  144.8 2.3 convolution_add_fusion.8
  149.8 1.5 copy.140
  151.3 3.4 fusion.167
  154.6 1.5 copy.141
  158.9 2.3 fusion.168
  178.7 2.2 exponential_multiply_fusion.2
  181.0 1.1 fusion.164
  182.6 1.2 convert_bitcast_fusion.2
  185.1 1.5 rsqrt_multiply_fusion.2
  186.5 1.8 fusion.171
  188.4 1.2 multiply_convert_fusion.2
  191.1 2.3 convolution_add_fusion.8
  196.1 1.5 copy.140
  197.6 3.4 fusion.167
  200.9 1.5 copy.141
  205.2 2.3 fusion.168
  225.0 2.2 exponential_multiply_fusion.2
  227.3 1.1 fusion.164
  228.9 1.2 convert_bitcast_fusion.2
  231.3 1.5 rsqrt_multiply_fusion.2
  232.8 1.8 fusion.171
  234.7 1.2 multiply_convert_fusion.2
  237.4 2.3 convolution_add_fusion.8
  240.0 1.1 convolution_add_fusion.7
  242.4 1.5 copy.140
  243.9 3.4 fusion.167
  247.2 1.5 copy.141
  251.5 2.3 fusion.168
  256.6 1.1 copy.80
  257.8 25.3 %all_to_all.36 = f32[128,8,128]{2,1,0:T(8,128)S(1)} all-to-all(f32[128,8,128]{2,1,0:T(8,128)S(1)} %bitcast.322), channel_id=1, replica_groups=mesh['gs'=128,'view'=4] {'gs'}, dimensions={0} | all-to-all | bytes 1048576 | tf_op jit(solution)/shard_map/all_to_all | solution.py:132
  283.1 3.4 scatter_custom_fusion
  286.5 2.5 collective-permute-start
  288.9 11.8 %collective-permute-done = f32[1024,128]{1,0:T(8,128)S(1)} collective-permute-done((f32[1024,128]{1,0:T(8,128)S(1)}, f32[1024,128]{1,0:T(8,128)S(1)}, u32[]{:S(2)}, u32[]{:S(2)}) %collective-permute-start) | collective-permute-done | bytes 524320 | tf_op jit(solution)/shard_map/ppermute | solution.py:138
  300.8 3.0 collective-permute-start.1
  305.6 9.8 %all-to-all-start.3 = ((f32[9,128,8]{0,2,1:T(8,128)}), f32[9,128,8]{0,2,1:T(8,128)S(1)}, u32[]{:S(2)}, u32[]{:S(2)}) async-start(f32[9,128,8]{0,2,1:T(8,128)} %bitcast.13), calls=%async_computation.3 | async-start | bytes 1048576 | tf_op jit(solution)/shard_map/all_to_all | solution.py:131
  315.5 18.0 %all-to-all-done.3 = f32[9,128,8]{0,2,1:T(8,128)S(1)} async-done(((f32[9,128,8]{0,2,1:T(8,128)}), f32[9,128,8]{0,2,1:T(8,128)S(1)}, u32[]{:S(2)}, u32[]{:S(2)}) %all-to-all-start.3) | async-done | bytes 36896 | tf_op jit(solution)/shard_map/all_to_all | solution.py:131
  333.5 3.4 scatter_custom_fusion.1
  337.7 236.5 %all-reduce.11.cloned.1.call-done = f32[128,512]{1,0:T(8,128)} async-done(((f32[128,512]{1,0:T(8,128)}), f32[128,512]{1,0:T(8,128)}) %all-reduce.11.cloned.1.call-update) | async-done | bytes 262160 | tf_op jit(solution)/shard_map/psum | solution.py:141
  574.2 1.7 broadcast_multiply_fusion.2
  (502 shorter events, 93.4 us)
Async XLA Ops:
  7.2 24.6 %copy-start = (bf16[1024,128]{1,0:T(8,128)(2,1)S(1)}, bf16[1024,128]{1,0:T(8,128)(2,1)}, u32[]{:S(2)}) copy-start(bf16[1024,128]{1,0:T(8,128)(2,1)} %param.10) | copy-start | bytes 786436
  14.1 35.6 %all-to-all-start = ((f32[9,128,8]{0,2,1:T(8,128)}), f32[9,128,8]{0,2,1:T(8,128)S(1)}, u32[]{:S(2)}, u32[]{:S(2)}) async-start(f32[9,128,8]{0,2,1:T(8,128)} %bitcast_select_fusion.1), calls=%async_computation | async-start | bytes 1048576 | tf_op jit(solution)/shard_map/all_to_all | solution.py:118
  49.6 22.1 %all-to-all-start.1 = ((bf16[128,8,128]{2,1,0:T(8,128)(2,1)}), bf16[128,8,128]{2,1,0:T(8,128)(2,1)S(1)}, u32[]{:S(2)}, u32[]{:S(2)}) async-start(bf16[128,8,128]{2,1,0:T(8,128)(2,1)} %bitcast_select_fusion.2), calls=%async_computation.1 | async-start | bytes 524288 | tf_op jit(solution)/shard_map/all_to_all | solution.py:120
  58.5 515.6 %all-reduce.11.cloned.1.call-start = ((), (), s32[]{:S(2)}) async-start(), calls=%async_computation.4 | async-start | bytes 524288 | tf_op jit(solution)/shard_map/psum | solution.py:141
  72.3 10.4 %copy-start.21 = (f32[9,8,128]{2,0,1:T(8,128)}, f32[9,8,128]{2,0,1:T(8,128)S(1)}, u32[]{:S(2)}) copy-start(f32[9,8,128]{2,0,1:T(8,128)S(1)} %get-tuple-element.840) | copy-start | bytes 110596 | tf_op jit(solution)/shard_map/while
  72.3 12.9 %copy-start.8 = (bf16[8,128,128]{2,1,0:T(8,128)(2,1)}, bf16[8,128,128]{2,1,0:T(8,128)(2,1)S(1)}, u32[]{:S(2)}) copy-start(bf16[8,128,128]{2,1,0:T(8,128)(2,1)S(1)} %get-tuple-element.843) | copy-start | bytes 786436 | tf_op jit(solution)/shard_map/while
  80.1 22.1 %copy-start.23 = (f32[256]{0:T(256)}, f32[256]{0:T(256)S(1)}, u32[]{:S(2)}) copy-start(f32[256]{0:T(256)S(1)} %get-tuple-element.768) | copy-start | bytes 3076 | tf_op jit(solution)/shard_map/while
  80.1 22.2 %copy-start.25 = (f32[256]{0:T(256)}, f32[256]{0:T(256)S(1)}, u32[]{:S(2)}) copy-start(f32[256]{0:T(256)S(1)} %get-tuple-element.765) | copy-start | bytes 3076 | tf_op jit(solution)/shard_map/while
  80.8 18.8 %copy-start.30 = (s32[8]{0:T(128)}, s32[8]{0:T(128)S(1)}, u32[]{:S(2)}) copy-start(s32[8]{0:T(128)S(1)} %get-tuple-element.785) | copy-start | bytes 100 | tf_op jit(solution)/shard_map/while
  82.1 19.0 %copy-start.5 = (f32[9,8,128]{2,0,1:T(8,128)}, f32[9,8,128]{2,0,1:T(8,128)S(1)}, u32[]{:S(2)}) copy-start(f32[9,8,128]{2,0,1:T(8,128)S(1)} %select_bitcast_fusion.2) | copy-start | bytes 110596 | tf_op jit(solution)/shard_map/while
  82.8 19.4 %copy-start.11 = (f32[1,8,128]{2,0,1:T(1,128)}, f32[1,8,128]{2,0,1:T(1,128)S(1)}, u32[]{:S(2)}) copy-start(f32[1,8,128]{2,0,1:T(1,128)S(1)} %get-tuple-element.769) | copy-start | bytes 12292 | tf_op jit(solution)/shard_map/while
  83.4 18.9 %copy-start.16 = (f32[1024]{0:T(1024)}, f32[1024]{0:T(1024)S(1)}, u32[]{:S(2)}) copy-start(f32[1024]{0:T(1024)S(1)} %bitcast_multiply_fusion.8) | copy-start | bytes 12292 | tf_op jit(solution)/shard_map/while
  112.6 2.3 copy-start.28
  112.6 2.4 copy-start.29
  112.6 3.3 copy-start.27
  114.9 2.6 copy-start.9
  117.6 10.4 %copy-start.21 = (f32[9,8,128]{2,0,1:T(8,128)}, f32[9,8,128]{2,0,1:T(8,128)S(1)}, u32[]{:S(2)}) copy-start(f32[9,8,128]{2,0,1:T(8,128)S(1)} %get-tuple-element.840) | copy-start | bytes 110596 | tf_op jit(solution)/shard_map/while
  117.6 12.9 %copy-start.8 = (bf16[8,128,128]{2,1,0:T(8,128)(2,1)}, bf16[8,128,128]{2,1,0:T(8,128)(2,1)S(1)}, u32[]{:S(2)}) copy-start(bf16[8,128,128]{2,1,0:T(8,128)(2,1)S(1)} %get-tuple-element.843) | copy-start | bytes 786436 | tf_op jit(solution)/shard_map/while
  125.3 23.2 %copy-start.23 = (f32[256]{0:T(256)}, f32[256]{0:T(256)S(1)}, u32[]{:S(2)}) copy-start(f32[256]{0:T(256)S(1)} %get-tuple-element.768) | copy-start | bytes 3076 | tf_op jit(solution)/shard_map/while
  125.3 23.2 %copy-start.25 = (f32[256]{0:T(256)}, f32[256]{0:T(256)S(1)}, u32[]{:S(2)}) copy-start(f32[256]{0:T(256)S(1)} %get-tuple-element.765) | copy-start | bytes 3076 | tf_op jit(solution)/shard_map/while
  126.0 18.8 %copy-start.30 = (s32[8]{0:T(128)}, s32[8]{0:T(128)S(1)}, u32[]{:S(2)}) copy-start(s32[8]{0:T(128)S(1)} %get-tuple-element.785) | copy-start | bytes 100 | tf_op jit(solution)/shard_map/while
  127.3 20.1 %copy-start.5 = (f32[9,8,128]{2,0,1:T(8,128)}, f32[9,8,128]{2,0,1:T(8,128)S(1)}, u32[]{:S(2)}) copy-start(f32[9,8,128]{2,0,1:T(8,128)S(1)} %select_bitcast_fusion.2) | copy-start | bytes 110596 | tf_op jit(solution)/shard_map/while
  128.0 20.5 %copy-start.11 = (f32[1,8,128]{2,0,1:T(1,128)}, f32[1,8,128]{2,0,1:T(1,128)S(1)}, u32[]{:S(2)}) copy-start(f32[1,8,128]{2,0,1:T(1,128)S(1)} %get-tuple-element.769) | copy-start | bytes 12292 | tf_op jit(solution)/shard_map/while
  128.6 20.0 %copy-start.16 = (f32[1024]{0:T(1024)}, f32[1024]{0:T(1024)S(1)}, u32[]{:S(2)}) copy-start(f32[1024]{0:T(1024)S(1)} %bitcast_multiply_fusion.8) | copy-start | bytes 12292 | tf_op jit(solution)/shard_map/while
  144.5 2.6 copy-start.7
  144.8 2.3 copy-start.4
  158.9 2.3 copy-start.15
  158.9 2.3 copy-start.28
  158.9 2.4 copy-start.29
  158.9 3.3 copy-start.27
  161.2 2.6 copy-start.9
  163.8 10.4 %copy-start.21 = (f32[9,8,128]{2,0,1:T(8,128)}, f32[9,8,128]{2,0,1:T(8,128)S(1)}, u32[]{:S(2)}) copy-start(f32[9,8,128]{2,0,1:T(8,128)S(1)} %get-tuple-element.840) | copy-start | bytes 110596 | tf_op jit(solution)/shard_map/while
  163.9 12.9 %copy-start.8 = (bf16[8,128,128]{2,1,0:T(8,128)(2,1)}, bf16[8,128,128]{2,1,0:T(8,128)(2,1)S(1)}, u32[]{:S(2)}) copy-start(bf16[8,128,128]{2,1,0:T(8,128)(2,1)S(1)} %get-tuple-element.843) | copy-start | bytes 786436 | tf_op jit(solution)/shard_map/while
  171.5 23.2 %copy-start.23 = (f32[256]{0:T(256)}, f32[256]{0:T(256)S(1)}, u32[]{:S(2)}) copy-start(f32[256]{0:T(256)S(1)} %get-tuple-element.768) | copy-start | bytes 3076 | tf_op jit(solution)/shard_map/while
  171.5 23.2 %copy-start.25 = (f32[256]{0:T(256)}, f32[256]{0:T(256)S(1)}, u32[]{:S(2)}) copy-start(f32[256]{0:T(256)S(1)} %get-tuple-element.765) | copy-start | bytes 3076 | tf_op jit(solution)/shard_map/while
  172.3 18.8 %copy-start.30 = (s32[8]{0:T(128)}, s32[8]{0:T(128)S(1)}, u32[]{:S(2)}) copy-start(s32[8]{0:T(128)S(1)} %get-tuple-element.785) | copy-start | bytes 100 | tf_op jit(solution)/shard_map/while
  173.6 20.1 %copy-start.5 = (f32[9,8,128]{2,0,1:T(8,128)}, f32[9,8,128]{2,0,1:T(8,128)S(1)}, u32[]{:S(2)}) copy-start(f32[9,8,128]{2,0,1:T(8,128)S(1)} %select_bitcast_fusion.2) | copy-start | bytes 110596 | tf_op jit(solution)/shard_map/while
  174.3 20.5 %copy-start.11 = (f32[1,8,128]{2,0,1:T(1,128)}, f32[1,8,128]{2,0,1:T(1,128)S(1)}, u32[]{:S(2)}) copy-start(f32[1,8,128]{2,0,1:T(1,128)S(1)} %get-tuple-element.769) | copy-start | bytes 12292 | tf_op jit(solution)/shard_map/while
  174.9 20.0 %copy-start.16 = (f32[1024]{0:T(1024)}, f32[1024]{0:T(1024)S(1)}, u32[]{:S(2)}) copy-start(f32[1024]{0:T(1024)S(1)} %bitcast_multiply_fusion.8) | copy-start | bytes 12292 | tf_op jit(solution)/shard_map/while
  190.8 2.6 copy-start.7
  191.1 2.3 copy-start.4
  205.2 2.3 copy-start.15
  205.2 2.3 copy-start.28
  205.2 2.4 copy-start.29
  205.2 3.3 copy-start.27
  207.5 2.6 copy-start.9
  210.1 10.4 %copy-start.21 = (f32[9,8,128]{2,0,1:T(8,128)}, f32[9,8,128]{2,0,1:T(8,128)S(1)}, u32[]{:S(2)}) copy-start(f32[9,8,128]{2,0,1:T(8,128)S(1)} %get-tuple-element.840) | copy-start | bytes 110596 | tf_op jit(solution)/shard_map/while
  210.1 12.9 %copy-start.8 = (bf16[8,128,128]{2,1,0:T(8,128)(2,1)}, bf16[8,128,128]{2,1,0:T(8,128)(2,1)S(1)}, u32[]{:S(2)}) copy-start(bf16[8,128,128]{2,1,0:T(8,128)(2,1)S(1)} %get-tuple-element.843) | copy-start | bytes 786436 | tf_op jit(solution)/shard_map/while
  217.8 23.2 %copy-start.23 = (f32[256]{0:T(256)}, f32[256]{0:T(256)S(1)}, u32[]{:S(2)}) copy-start(f32[256]{0:T(256)S(1)} %get-tuple-element.768) | copy-start | bytes 3076 | tf_op jit(solution)/shard_map/while
  217.8 23.3 %copy-start.25 = (f32[256]{0:T(256)}, f32[256]{0:T(256)S(1)}, u32[]{:S(2)}) copy-start(f32[256]{0:T(256)S(1)} %get-tuple-element.765) | copy-start | bytes 3076 | tf_op jit(solution)/shard_map/while
  218.5 18.8 %copy-start.30 = (s32[8]{0:T(128)}, s32[8]{0:T(128)S(1)}, u32[]{:S(2)}) copy-start(s32[8]{0:T(128)S(1)} %get-tuple-element.785) | copy-start | bytes 100 | tf_op jit(solution)/shard_map/while
  219.9 20.1 %copy-start.5 = (f32[9,8,128]{2,0,1:T(8,128)}, f32[9,8,128]{2,0,1:T(8,128)S(1)}, u32[]{:S(2)}) copy-start(f32[9,8,128]{2,0,1:T(8,128)S(1)} %select_bitcast_fusion.2) | copy-start | bytes 110596 | tf_op jit(solution)/shard_map/while
  220.6 20.5 %copy-start.11 = (f32[1,8,128]{2,0,1:T(1,128)}, f32[1,8,128]{2,0,1:T(1,128)S(1)}, u32[]{:S(2)}) copy-start(f32[1,8,128]{2,0,1:T(1,128)S(1)} %get-tuple-element.769) | copy-start | bytes 12292 | tf_op jit(solution)/shard_map/while
  221.2 20.0 %copy-start.16 = (f32[1024]{0:T(1024)}, f32[1024]{0:T(1024)S(1)}, u32[]{:S(2)}) copy-start(f32[1024]{0:T(1024)S(1)} %bitcast_multiply_fusion.8) | copy-start | bytes 12292 | tf_op jit(solution)/shard_map/while
  237.1 2.6 copy-start.7
  237.4 2.3 copy-start.4
  251.5 2.3 copy-start.15
  251.5 2.3 copy-start.28
  251.5 2.4 copy-start.29
  251.5 3.3 copy-start.27
  253.8 2.6 copy-start.9
  286.5 14.2 %collective-permute-start = (f32[1024,128]{1,0:T(8,128)S(1)}, f32[1024,128]{1,0:T(8,128)S(1)}, u32[]{:S(2)}, u32[]{:S(2)}) collective-permute-start(f32[1024,128]{1,0:T(8,128)S(1)} %scatter_custom_fusion), channel_id=1, source_target_pairs={{0,1},{1,0},{2,3},{3,2},{4,5},{5,4},{6,7},{7,6},{8,9},{9,8},{10,11... | collective-permute-start | bytes 1572872 | tf_op jit(solution)/shard_map/ppermute | solution.py:138
  300.8 275.1 %collective-permute-start.1 = (f32[1024,128]{1,0:T(8,128)S(1)}, f32[1024,128]{1,0:T(8,128)S(1)}, u32[]{:S(2)}, u32[]{:S(2)}) collective-permute-start(f32[1024,128]{1,0:T(8,128)S(1)} %add.471), channel_id=1, source_target_pairs={{0,2},{1,3},{2,0},{3,1},{4,6},{5,7},{6,4},{7,5},{8,10},{9,11},{10,... | collective-permute-start | bytes 1572872 | tf_op jit(solution)/shard_map/ppermute | solution.py:138
  305.6 27.9 %all-to-all-start.3 = ((f32[9,128,8]{0,2,1:T(8,128)}), f32[9,128,8]{0,2,1:T(8,128)S(1)}, u32[]{:S(2)}, u32[]{:S(2)}) async-start(f32[9,128,8]{0,2,1:T(8,128)} %bitcast.13), calls=%async_computation.3 | async-start | bytes 1048576 | tf_op jit(solution)/shard_map/all_to_all | solution.py:131
  (81 other events, 83.0 us)
Sparse Core Ops, SparseCore 0:
  304.0 270.1 all-reduce.10
